TPU v7x, 32 devices: a whole 2x2x4 slice. The times are simulated.
32 devices in a mesh: dp: 2 (over x), space: 16 (over z, y, core).
Axes of the slice: x: 2, y: 2, z: 4, core: 2. Of those that a mesh axis runs over, the one named last changes fastest.
Arguments:
- tiles_in: bfloat16 [2, 64, 8, 8, 384], P('dp', 'space'), may hold values from -6 to 6
- upstream: bfloat16 [2, 64, 8, 8, 384], P('dp', 'space'), may hold values from -1.1953125 to 1.1953125
- pool_weight: float32 [2, 64], P('dp', 'space'), may hold values from 0.25 to 4
- slide_cot: float32 [2, 384], P('dp'), may hold values from -6 to 6
- adjacency: int32 [2, 64, 8], P('dp', 'space'), may hold values from -1 to 63, as said below
- counts: int32 [2, 16], P('dp', 'space'), may hold values from 1 to 4, as said below
- kernel: float32 [7, 7, 384], replicated, may hold values from -0.875 to 0.875
- norm_gain: float32 [384], replicated, may hold values from 0.5 to 1.5
- w_in: bfloat16 [384, 1536], replicated, may hold values from -0.3125 to 0.3125
- w_out: bfloat16 [1536, 384], replicated, may hold values from -0.15625 to 0.15625
- layer_scale: float32 [384], replicated, may hold values from 0.1 to 1
Outputs:
- embedding: float32 [2, 384], P('dp')
- grad_tiles: bfloat16 [2, 64, 8, 8, 384], P('dp', 'space')
- grad_w_out: float32 [1536, 384], P('space')
- grad_kernel: float32 [7, 7, 384], replicated
Inputs may be any that keep to these rules, and one draw needn't show every extreme that they name: Slots form blocks of 4; block k of a slide is one row of tiles, its live tiles in its first counts slots in column order; the last block of every slide is full, and often another one too. `adjacency`: tiles lie on a grid: entries 0, 4, 5 name live slots of the block before the tile's own, entries 1, 6, 7 of the block after it, entries 2 and 3 of its own block. The lists are mutual (b is the north neighbour of a exactly when a is the south neighbour of b, and likewise for the other directions). Slots that are not live have no neighbours and are named by none.
All inputs are finite; a program needn't handle non-finite values.
Results may differ from a plain program's by a relative error of at most 0.011.
Values may be sent and summed in bfloat16 or wider, within the bound.
No kernel may reach another device: no remote copies, remote signals or barrier semaphores. Data moves between devices by JAX's collectives and lax.ppermute only.
A program may use at most 64 MiB of HBM per device.

v0:
```python
import jax
import jax.numpy as jnp
from jax import lax
from jax.sharding import PartitionSpec as P

sqrt_half = 0.7071067811865476
inv_root_two_pi = 0.3989422804014327


def passed_along(value, axis, steps):
    count = lax.axis_size(axis)
    leading, last = (max(0, -steps), min(count, count - steps))
    return lax.ppermute(value, axis, [(source, source + steps) for source in range(leading, last)])


def depthwise(padded, kernel, tile_side):
    total = jnp.zeros(padded.shape[:1] + (tile_side, tile_side, padded.shape[3]), jnp.float32)
    for row_tap in range(7):
        for col_tap in range(7):
            window = padded[
                :, row_tap : row_tap + tile_side, col_tap : col_tap + tile_side, :
            ].astype(jnp.float32)
            total = total + window * kernel[row_tap, col_tap]
    return total


def pick(source, wanted, offset):
    valid = wanted >= 0
    index = jnp.clip(wanted - offset, 0, source.shape[0] - 1)
    chosen = jnp.take(source, index, axis=0)
    return jnp.where(valid[:, None, None, None], chosen, jnp.zeros_like(chosen))


def frame(
    own, north_rows, south_rows, right_cols, left_cols, wanted, north_base, own_base, south_base
):
    tile_side = own.shape[1]
    upper = jnp.concatenate(
        [
            pick(north_rows, wanted[:, 4], north_base)[:, :, tile_side - 3 :],
            pick(north_rows, wanted[:, 0], north_base),
            pick(north_rows, wanted[:, 5], north_base)[:, :, :3],
        ],
        axis=2,
    )
    middle = jnp.concatenate(
        [pick(right_cols, wanted[:, 2], own_base), own, pick(left_cols, wanted[:, 3], own_base)],
        axis=2,
    )
    lower = jnp.concatenate(
        [
            pick(south_rows, wanted[:, 6], south_base)[:, :, tile_side - 3 :],
            pick(south_rows, wanted[:, 1], south_base),
            pick(south_rows, wanted[:, 7], south_base)[:, :, :3],
        ],
        axis=2,
    )
    return jnp.concatenate([upper, middle, lower], axis=1)


def block_pass(
    padded, own, upstream, pool_weight, live, slide_cot, kernel, norm_gain, w_in, w_out, layer_scale
):
    tile_side = own.shape[1]
    channels = own.shape[3]
    conv_out = depthwise(padded, kernel, tile_side)
    centred = conv_out - jnp.mean(conv_out, axis=-1, keepdims=True)
    inv_std = lax.rsqrt(jnp.mean(centred * centred, axis=-1, keepdims=True) + 1e-06)
    normed = centred * inv_std
    lifted = (normed * norm_gain).astype(jnp.bfloat16).reshape(-1, channels)
    pre = jnp.dot(lifted, w_in, preferred_element_type=jnp.float32)
    cdf = 0.5 * (1.0 + jax.scipy.special.erf(pre * sqrt_half))
    activated = (pre * cdf).astype(jnp.bfloat16)
    mixed = jnp.dot(activated, w_out, preferred_element_type=jnp.float32).reshape(own.shape)
    block_out = own.astype(jnp.float32) + layer_scale * mixed
    weight_live = live * pool_weight
    emb_term = jnp.sum(weight_live[:, None] * jnp.sum(block_out, axis=(1, 2)), axis=0) / tile_side
    extra = pool_weight[:, None] * slide_cot[None, :] / tile_side
    grad_out = live[:, None, None, None] * (upstream.astype(jnp.float32) + extra[:, None, None, :])
    grad_mixed = (grad_out * layer_scale).astype(jnp.bfloat16).reshape(-1, channels)
    grad_act = lax.dot_general(
        grad_mixed, w_out, (((1,), (1,)), ((), ())), preferred_element_type=jnp.float32
    )
    density = jnp.exp(-0.5 * pre * pre) * inv_root_two_pi
    grad_pre = (grad_act * (cdf + pre * density)).astype(jnp.bfloat16)
    grad_lift = lax.dot_general(
        grad_pre, w_in, (((1,), (1,)), ((), ())), preferred_element_type=jnp.float32
    )
    grad_normed = grad_lift.reshape(own.shape) * norm_gain
    grad_conv = inv_std * (
        grad_normed
        - jnp.mean(grad_normed, axis=-1, keepdims=True)
        - normed * jnp.mean(grad_normed * normed, axis=-1, keepdims=True)
    )
    kernel_rows = []
    for row_tap in range(7):
        for col_tap in range(7):
            window = padded[
                :, row_tap : row_tap + tile_side, col_tap : col_tap + tile_side, :
            ].astype(jnp.float32)
            kernel_rows.append(jnp.sum(window * grad_conv, axis=(0, 1, 2)))
    kernel_grad = jnp.stack(kernel_rows).reshape(7, 7, channels)
    return (emb_term, grad_out, grad_conv, activated, grad_mixed, kernel_grad)


def per_device(
    tiles_in,
    upstream,
    pool_weight,
    slide_cot,
    adjacency,
    counts,
    kernel,
    norm_gain,
    w_in,
    w_out,
    layer_scale,
):
    own = tiles_in[0]
    capacity = own.shape[0]
    tile_side = own.shape[1]
    position = lax.axis_index("space")
    own_base = position * capacity
    north_base = own_base - capacity
    south_base = own_base + capacity
    wanted = adjacency[0]
    live = (jnp.arange(capacity, dtype=jnp.int32) < counts[0, 0]).astype(jnp.float32)
    north_rows = passed_along(own[:, tile_side - 3 :], "space", 1)
    south_rows = passed_along(own[:, :3], "space", -1)
    padded = frame(
        own,
        north_rows,
        south_rows,
        own[:, :, tile_side - 3 :],
        own[:, :, :3],
        wanted,
        north_base,
        own_base,
        south_base,
    )
    emb_term, grad_out, grad_conv, activated, grad_mixed, kernel_grad = block_pass(
        padded,
        own,
        upstream[0],
        pool_weight[0],
        live,
        slide_cot[0],
        kernel,
        norm_gain,
        w_in,
        w_out,
        layer_scale,
    )
    embedding = lax.psum(emb_term, "space")
    local_weight = lax.dot_general(
        activated, grad_mixed, (((0,), (0,)), ((), ())), preferred_element_type=jnp.float32
    )
    whole_weight, kernel_dp = (
        lax.psum(local_weight.astype(jnp.bfloat16), "dp").astype(jnp.float32),
        lax.psum(kernel_grad.astype(jnp.bfloat16), "dp").astype(jnp.float32),
    )
    weight_share = lax.psum_scatter(whole_weight, "space", scatter_dimension=0, tiled=True)
    kernel_total = lax.psum(kernel_dp, "space")
    grad_north = passed_along(
        grad_conv[:, tile_side - 3 :].astype(jnp.bfloat16), "space", 1
    ).astype(jnp.float32)
    grad_south = passed_along(grad_conv[:, :3].astype(jnp.bfloat16), "space", -1).astype(
        jnp.float32
    )
    padded_grad = frame(
        grad_conv,
        grad_north,
        grad_south,
        grad_conv[:, :, tile_side - 3 :],
        grad_conv[:, :, :3],
        wanted,
        north_base,
        own_base,
        south_base,
    )
    back = depthwise(padded_grad, kernel[::-1, ::-1], tile_side)
    grad_tiles = ((grad_out + back) * live[:, None, None, None]).astype(jnp.bfloat16)
    return (embedding[None, :], grad_tiles[None], weight_share, kernel_total)


def solution(mesh):
    return jax.shard_map(
        per_device,
        mesh=mesh,
        in_specs=(
            P("dp", "space", None, None, None),
            P("dp", "space", None, None, None),
            P("dp", "space"),
            P("dp", None),
            P("dp", "space", None),
            P("dp", "space"),
            P(),
            P(),
            P(),
            P(),
            P(),
        ),
        out_specs=(P("dp", None), P("dp", "space", None, None, None), P("space", None), P()),
        check_vma=False,
    )
```

profile of v0, /device:TPU:0, one launch (start us, length us, event | category | flops | bytes accessed | tf_op | source)
XLA Modules:
  0.0 189.6 jit_solution(16808455452502542343)
XLA Ops:
  7.2 1.0 fusion.191
  8.3 2.4 %collective-permute-start = (bf16[4,3,8,384]{3,2,1,0:T(8,128)(2,1)S(1)}, bf16[4,3,8,384]{3,2,1,0:T(8,128)(2,1)S(1)}, u32[]{:S(2)}, u32[]{:S(2)}) collective-permute-start(bf16[4,3,8,384]{3,2,1,0:T(8,128)(2,1)S(1)} %get-tuple-element.146), channel_id=1, source_target_pairs={{0,1},{1,2},{2,3},{3,4},{4,5},{5,6},{6,7},{7,8},{8,9},{9,10},{10,1... | collective-permute-start | bytes 221192 | tf_op jit(solution)/shard_map/ppermute | solution.py:13
  10.7 1.3 collective-permute-start.1
  12.0 1.1 fusion.192
  13.1 1.3 compare_reduce_fusion.7
  14.5 1.3 clamp_reduce_fusion.7
  15.9 0.6 compare_and_fusion.4
  16.5 0.6 compare_and_fusion.2
  17.1 1.0 slice_reduce_fusion.46
  18.1 1.9 %slice_reduce_fusion.48 = (f32[384]{0:T(512)S(1)}, f32[384]{0:T(512)S(1)}, f32[384]{0:T(512)S(1)}, f32[384]{0:T(512)S(1)}, f32[384]{0:T(512)S(1)}, /*index=5*/f3...) fusion(f32[7,7,384]{2,1,0:T(8,128)} %param.25), kind=kLoop, calls=%fused_computation.487 | loop fusion | bytes 58368 | tf_op jit(solution)/shard_map/slice | solution.py:23
  20.1 1.9 slice_reduce_fusion.47
  23.0 0.7 reduce.66
  23.7 1.2 compare_select_fusion.8
  24.8 0.7 multiply_multiply_fusion.1
  25.6 0.6 gather_fusion.4
  26.2 0.6 gather_fusion.3
  26.9 0.8 select_select_fusion.4
  27.7 0.8 select_select_fusion.5
  28.5 0.8 fusion.169
  29.3 0.6 gather_fusion.2
  29.9 0.8 fusion.182
  30.7 0.6 gather_fusion.1
  31.3 0.6 gather_fusion
  32.0 0.6 gather_fusion.7
  32.8 0.6 gather_fusion.6
  33.5 0.6 gather_fusion.5
  34.1 0.8 fusion.181
  34.9 0.4 maximum_maximum_fusion.2
  35.5 4.3 %fusion.187 = (f32[4,8,8]{2,1,0:T(8,128)S(1)}, f32[4,8,8,384]{3,2,1,0:T(8,128)S(1)}) fusion(f32[384]{0:T(512)S(1)} %get-tuple-element.114, bf16[4,11,14,384]{3,2,1,0:T(8,128)(2,1)S(1)} %get-tuple-element.143, f32[384]{0:T(512)S(1)} %get-tuple-element.115, f32[384]{0:T(512)S(1)} %get-tuple-element.68, f32[384]{0:T(512)S(1)} %get-tuple-element.69, ...), kind=kLoop, calls=%fused_computation.495 | loop fusion | flops 16219904 | bytes 9071104 | tf_op jit(solution)/shard_map/reduce_sum | solution.py:67
  39.8 0.2 multiply_reduce_fusion.2
  40.1 0.1 multiply_convert_fusion.1
  40.2 2.0 %multiply_convert_fusion = (bf16[256,1536]{1,0:T(8,128)(2,1)}, f32[256,1536]{1,0:T(8,128)}) fusion(bf16[256,384]{1,0:T(8,128)(2,1)S(1)} %bitcast.50, bf16[384,1536]{1,0:T(8,128)(2,1)S(1)} %copy-done), kind=kOutput, calls=%fused_computation.24 | convolution fusion | flops 303955968 | bytes 3735552 | tf_op jit(solution)/shard_map/dot_general | solution.py:71
  42.2 3.1 %multiply_reduce_fusion.1 = (f32[256]{0:T(256)S(1)}, f32[256,384]{1,0:T(8,128)S(1)}) fusion(f32[384]{0:T(512)S(1)} %copy-done.7, bf16[384,1536]{1,0:T(8,128)(2,1)S(1)} %copy-done, bf16[256,384]{1,0:T(8,128)(2,1)} %fusion.169, bf16[1536,384]{1,0:T(8,128)(2,1)} %param.28, f32[256,1536]{1,0:T(8,128)} %get-tuple-element.153), kind=kOutput, calls=%fused_computation.359 | convolution fusion | flops 608108288 | bytes 4524544 | tf_op jit(solution)/shard_map/dot_general | solution.py:86
  45.3 0.2 multiply_reduce_fusion
  45.7 2.8 %convolution_convert_fusion = bf16[1536,384]{1,0:T(8,128)(2,1)} fusion(bf16[256,1536]{1,0:T(8,128)(2,1)} %get-tuple-element.152, bf16[256,384]{1,0:T(8,128)(2,1)} %fusion.169), kind=kOutput, calls=%fused_computation.16 | convolution fusion | flops 302579712 | bytes 2162688 | tf_op jit(solution)/shard_map/dot_general | solution.py:155
  48.6 2.0 %fusion.186 = (bf16[4,8,8,384]{3,2,1,0:T(8,128)(2,1)}, f32[4,8,8,384]{3,2,1,0:T(8,128)S(1)}) fusion(f32[4,8,8]{2,1,0:T(8,128)S(1)} %broadcast_multiply_fusion, f32[4,8,8,384]{3,2,1,0:T(8,128)S(1)} %get-tuple-element.137, f32[4,8,8]{2,1,0:T(8,128)S(1)} %broadcast_multiply_fusion.1, f32[4,8,8]{2,1,0:T(8,128)S(1)} %div.33, f32[384]{0:T(512)S(1)} %copy-done.7, ...), kind=kLoop, calls=%fused_computation.494 | loop fusion | flops 786432 | bytes 1381888 | tf_op jit(solution)/shard_map/convert.101
  50.5 3.1 %fusion.85 = (bf16[384]{0:T(512)(128)(2,1)}, bf16[384]{0:T(512)(128)(2,1)}, bf16[384]{0:T(512)(128)(2,1)}, bf16[384]{0:T(512)(128)(2,1)}, bf16[384]{0:T(512)(128...) fusion(f32[4,8,8,384]{3,2,1,0:T(8,128)S(1)} %get-tuple-element., ...), kind=kOutput, calls=%fused_computation.225 | convolution fusion | flops 306998016 | bytes 3505152 | tf_op jit(solution)/shard_map/dot_general | solution.py:74
  53.7 0.9 gather_fusion.12
  54.6 0.8 gather_fusion.11
  55.4 0.6 fusion.190
  56.1 5.1 %collective-permute-start.2 = (bf16[4,3,8,384]{3,2,1,0:T(8,128)(2,1)}, bf16[4,3,8,384]{3,2,1,0:T(8,128)(2,1)S(1)}, u32[]{:S(2)}, u32[]{:S(2)}) collective-permute-start(bf16[4,3,8,384]{3,2,1,0:T(8,128)(2,1)} %get-tuple-element.144), channel_id=1, source_target_pairs={{0,1},{1,2},{2,3},{3,4},{4,5},{5,6},{6,7},{7,8},{8,9},{9,10},{10,1... | collective-permute-start | bytes 221192 | tf_op jit(solution)/shard_map/ppermute | solution.py:13
  61.2 1.5 collective-permute-start.3
  62.7 0.7 multiply_reduce_fusion.3
  63.4 0.8 select_select_fusion
  64.2 0.8 select_select_fusion.1
  65.0 31.3 %all-reduce.4.cloned.1.call-done = bf16[1536,384]{1,0:T(8,128)(2,1)} async-done(((bf16[1536,384]{1,0:T(8,128)(2,1)}), bf16[1536,384]{1,0:T(8,128)(2,1)}) %all-reduce.4.cloned.1.call-update) | async-done | bytes 1179664 | tf_op jit(solution)/shard_map/psum | solution.py:159
  96.2 2.8 %convert_element_type.315 = f32[1536,384]{1,0:T(8,128)} convert(bf16[1536,384]{1,0:T(8,128)(2,1)} %all-reduce.4.cloned.1.call-done) | non-fusion elementwise | flops 589824 | bytes 3538944 | tf_op jit(solution)/shard_map/convert_element_type | solution.py:159
  99.1 1.0 fusion.53
  100.2 1.0 fusion.103
  101.2 0.2 fusion.35
  102.0 0.3 stack.249
  102.3 7.4 %psum.30 = bf16[7,7,384]{2,1,0:T(8,128)(2,1)S(1)} all-reduce(bf16[7,7,384]{2,1,0:T(8,128)(2,1)S(1)} %convert_element_type.316), channel_id=1, replica_groups=mesh['dp'=2,'space'=16] {'dp'}, use_global_device_ids=true, to_apply=%region_58.63 | all-reduce | flops 18816 | bytes 75264 | tf_op jit(solution)/shard_map/psum | solution.py:160
  109.8 61.0 %all-reduce.5 = (f32[1,384]{1,0:T(1,128)}, f32[7,7,384]{2,1,0:T(8,128)}) all-reduce(f32[1,384]{1,0:T(1,128)S(1)} %broadcast_in_dim.154, bf16[7,7,384]{2,1,0:T(8,128)(2,1)S(1)} %psum.30), channel_id=1, replica_groups=mesh['dp'=2,'space'=16] {'space'}, use_global_device_ids=true, to_apply=%region_4.7 | all-reduce | flops 19200 | bytes 115968 | tf_op jit(solution)/shard_map/psum | solution.py:154
  170.9 0.7 gather_fusion.10
  171.6 0.7 gather_fusion.9
  172.3 0.7 gather_fusion.8
  173.0 0.7 gather_fusion.15
  173.7 0.7 gather_fusion.14
  174.4 0.7 gather_fusion.13
  175.1 0.8 fusion.178
  176.1 0.8 fusion.177
  177.4 0.3 maximum_maximum_fusion
  177.7 0.3 copy-done.5
  178.3 4.4 %fusion.175 = bf16[1,4,8,8,384]{4,3,2,1,0:T(8,128)(2,1)} fusion(f32[384]{0:T(512)S(1)} %copy-done.19, f32[4,11,14,384]{3,2,1,0:T(8,128)S(1)} %get-tuple-element.139, f32[384]{0:T(512)S(1)} %copy-done.54, f32[384]{0:T(512)S(1)} %get-tuple-element.105, f32[384]{0:T(512)S(1)} %copy-done.13, f32[384]{0:T(512)S(1)} %copy-done.11, f32[384]{0:T(512)S(1)} %copy-done.9, ...), kind=kLoop, calls=%fused_computation.371 | loop fusion | flops 10715136 | bytes 17677840 | tf_op jit(solution)/shard_map/broadcast_in_dim | solution.py:183
  (318 shorter events, 2.0 us)
Async XLA Ops:
  7.2 33.0 %copy-start = (bf16[384,1536]{1,0:T(8,128)(2,1)S(1)}, bf16[384,1536]{1,0:T(8,128)(2,1)}, u32[]{:S(2)}) copy-start(bf16[384,1536]{1,0:T(8,128)(2,1)} %param.27) | copy-start | bytes 3538948
  7.2 21.3 %copy-start.69 = (f32[384]{0:T(512)S(1)}, f32[384]{0:T(512)}, u32[]{:S(2)}) copy-start(f32[384]{0:T(512)} %param.29) | copy-start | bytes 4612
  7.2 21.3 %copy-start.4 = (bf16[1,4,8,8,384]{4,3,2,1,0:T(8,128)(2,1)S(1)}, bf16[1,4,8,8,384]{4,3,2,1,0:T(8,128)(2,1)}, u32[]{:S(2)}) copy-start(bf16[1,4,8,8,384]{4,3,2,1,0:T(8,128)(2,1)} %param.20) | copy-start | bytes 589828
  7.2 89.0 %all-reduce.4.cloned.1.call-start = ((), (), s32[]{:S(2)}) async-start(), calls=%async_computation.1 | async-start | bytes 2359296 | tf_op jit(solution)/shard_map/psum | solution.py:159
  8.3 21.0 %collective-permute-start = (bf16[4,3,8,384]{3,2,1,0:T(8,128)(2,1)S(1)}, bf16[4,3,8,384]{3,2,1,0:T(8,128)(2,1)S(1)}, u32[]{:S(2)}, u32[]{:S(2)}) collective-permute-start(bf16[4,3,8,384]{3,2,1,0:T(8,128)(2,1)S(1)} %get-tuple-element.146), channel_id=1, source_target_pairs={{0,1},{1,2},{2,3},{3,4},{4,5},{5,6},{6,7},{7,8},{8,9},{9,10},{10,1... | collective-permute-start | bytes 221192 | tf_op jit(solution)/shard_map/ppermute | solution.py:13
  10.7 21.3 %collective-permute-start.1 = (bf16[4,3,8,384]{3,2,1,0:T(8,128)(2,1)S(1)}, bf16[4,3,8,384]{3,2,1,0:T(8,128)(2,1)S(1)}, u32[]{:S(2)}, u32[]{:S(2)}) collective-permute-start(bf16[4,3,8,384]{3,2,1,0:T(8,128)(2,1)S(1)} %get-tuple-element.147), channel_id=1, source_target_pairs={{1,0},{2,1},{3,2},{4,3},{5,4},{6,5},{7,6},{8,7},{9,8},{10,9},{11,1... | collective-permute-start | bytes 221192 | tf_op jit(solution)/shard_map/ppermute | solution.py:13
  14.4 18.2 %copy-start.81 = (pred[4]{0:T(512)(128)(4,1)}, pred[4]{0:T(512)(128)(4,1)S(1)}, u32[]{:S(2)}) copy-start(pred[4]{0:T(512)(128)(4,1)S(1)} %get-tuple-element.123) | copy-start | bytes 16
  14.4 18.2 %copy-start.87 = (pred[4]{0:T(512)(128)(4,1)}, pred[4]{0:T(512)(128)(4,1)S(1)}, u32[]{:S(2)}) copy-start(pred[4]{0:T(512)(128)(4,1)S(1)} %get-tuple-element.116) | copy-start | bytes 16
  14.4 18.2 %copy-start.89 = (pred[4]{0:T(512)(128)(4,1)}, pred[4]{0:T(512)(128)(4,1)S(1)}, u32[]{:S(2)}) copy-start(pred[4]{0:T(512)(128)(4,1)S(1)} %get-tuple-element.122) | copy-start | bytes 16
  14.4 18.2 %copy-start.91 = (pred[4]{0:T(512)(128)(4,1)}, pred[4]{0:T(512)(128)(4,1)S(1)}, u32[]{:S(2)}) copy-start(pred[4]{0:T(512)(128)(4,1)S(1)} %get-tuple-element.121) | copy-start | bytes 16
  14.5 18.2 %copy-start.92 = (pred[4]{0:T(512)(128)(4,1)}, pred[4]{0:T(512)(128)(4,1)S(1)}, u32[]{:S(2)}) copy-start(pred[4]{0:T(512)(128)(4,1)S(1)} %get-tuple-element.120) | copy-start | bytes 16
  14.5 18.2 %copy-start.85 = (pred[4]{0:T(512)(128)(4,1)}, pred[4]{0:T(512)(128)(4,1)S(1)}, u32[]{:S(2)}) copy-start(pred[4]{0:T(512)(128)(4,1)S(1)} %get-tuple-element.117) | copy-start | bytes 16
  14.5 18.9 %copy-start.79 = (pred[4]{0:T(512)(128)(4,1)}, pred[4]{0:T(512)(128)(4,1)S(1)}, u32[]{:S(2)}) copy-start(pred[4]{0:T(512)(128)(4,1)S(1)} %get-tuple-element.118) | copy-start | bytes 16
  14.5 19.6 %copy-start.83 = (pred[4]{0:T(512)(128)(4,1)}, pred[4]{0:T(512)(128)(4,1)S(1)}, u32[]{:S(2)}) copy-start(pred[4]{0:T(512)(128)(4,1)S(1)} %get-tuple-element.119) | copy-start | bytes 16
  15.8 16.9 %copy-start.97 = (pred[4]{0:T(512)(128)(4,1)}, pred[4]{0:T(512)(128)(4,1)S(1)}, u32[]{:S(2)}) copy-start(pred[4]{0:T(512)(128)(4,1)S(1)} %get-tuple-element.160) | copy-start | bytes 16
  15.8 17.6 %copy-start.93 = (pred[4]{0:T(512)(128)(4,1)}, pred[4]{0:T(512)(128)(4,1)S(1)}, u32[]{:S(2)}) copy-start(pred[4]{0:T(512)(128)(4,1)S(1)} %get-tuple-element.161) | copy-start | bytes 16
  15.9 16.8 %copy-start.95 = (pred[4]{0:T(512)(128)(4,1)}, pred[4]{0:T(512)(128)(4,1)S(1)}, u32[]{:S(2)}) copy-start(pred[4]{0:T(512)(128)(4,1)S(1)} %get-tuple-element.166) | copy-start | bytes 16
  15.9 16.8 %copy-start.99 = (pred[4]{0:T(512)(128)(4,1)}, pred[4]{0:T(512)(128)(4,1)S(1)}, u32[]{:S(2)}) copy-start(pred[4]{0:T(512)(128)(4,1)S(1)} %get-tuple-element.167) | copy-start | bytes 16
  18.0 17.3 %copy-start.8 = (f32[384]{0:T(512)}, f32[384]{0:T(512)S(1)}, u32[]{:S(2)}) copy-start(f32[384]{0:T(512)S(1)} %get-tuple-element.111) | copy-start | bytes 4612
  18.0 17.3 %copy-start.10 = (f32[384]{0:T(512)}, f32[384]{0:T(512)S(1)}, u32[]{:S(2)}) copy-start(f32[384]{0:T(512)S(1)} %get-tuple-element.112) | copy-start | bytes 4612
  18.1 17.3 %copy-start.12 = (f32[384]{0:T(512)}, f32[384]{0:T(512)S(1)}, u32[]{:S(2)}) copy-start(f32[384]{0:T(512)S(1)} %get-tuple-element.113) | copy-start | bytes 4612
  18.1 17.3 %copy-start.14 = (f32[384]{0:T(512)}, f32[384]{0:T(512)S(1)}, u32[]{:S(2)}) copy-start(f32[384]{0:T(512)S(1)} %get-tuple-element.114) | copy-start | bytes 4612
  18.1 17.3 %copy-start.16 = (f32[384]{0:T(512)}, f32[384]{0:T(512)S(1)}, u32[]{:S(2)}) copy-start(f32[384]{0:T(512)S(1)} %get-tuple-element.115) | copy-start | bytes 4612
  20.0 15.4 %copy-start.18 = (f32[384]{0:T(512)}, f32[384]{0:T(512)S(1)}, u32[]{:S(2)}) copy-start(f32[384]{0:T(512)S(1)} %get-tuple-element.67) | copy-start | bytes 4612
  20.0 15.4 %copy-start.20 = (f32[384]{0:T(512)}, f32[384]{0:T(512)S(1)}, u32[]{:S(2)}) copy-start(f32[384]{0:T(512)S(1)} %get-tuple-element.68) | copy-start | bytes 4612
  20.0 15.4 %copy-start.22 = (f32[384]{0:T(512)}, f32[384]{0:T(512)S(1)}, u32[]{:S(2)}) copy-start(f32[384]{0:T(512)S(1)} %get-tuple-element.69) | copy-start | bytes 4612
  20.0 15.4 %copy-start.24 = (f32[384]{0:T(512)}, f32[384]{0:T(512)S(1)}, u32[]{:S(2)}) copy-start(f32[384]{0:T(512)S(1)} %get-tuple-element.70) | copy-start | bytes 4612
  20.0 15.4 %copy-start.26 = (f32[384]{0:T(512)}, f32[384]{0:T(512)S(1)}, u32[]{:S(2)}) copy-start(f32[384]{0:T(512)S(1)} %get-tuple-element.71) | copy-start | bytes 4612
  20.0 15.4 %copy-start.28 = (f32[384]{0:T(512)}, f32[384]{0:T(512)S(1)}, u32[]{:S(2)}) copy-start(f32[384]{0:T(512)S(1)} %get-tuple-element.72) | copy-start | bytes 4612
  20.0 15.4 %copy-start.30 = (f32[384]{0:T(512)}, f32[384]{0:T(512)S(1)}, u32[]{:S(2)}) copy-start(f32[384]{0:T(512)S(1)} %get-tuple-element.73) | copy-start | bytes 4612
  20.0 15.4 %copy-start.32 = (f32[384]{0:T(512)}, f32[384]{0:T(512)S(1)}, u32[]{:S(2)}) copy-start(f32[384]{0:T(512)S(1)} %get-tuple-element.74) | copy-start | bytes 4612
  20.1 15.4 %copy-start.34 = (f32[384]{0:T(512)}, f32[384]{0:T(512)S(1)}, u32[]{:S(2)}) copy-start(f32[384]{0:T(512)S(1)} %get-tuple-element.75) | copy-start | bytes 4612
  20.1 15.4 %copy-start.36 = (f32[384]{0:T(512)}, f32[384]{0:T(512)S(1)}, u32[]{:S(2)}) copy-start(f32[384]{0:T(512)S(1)} %get-tuple-element.76) | copy-start | bytes 4612
  20.1 15.4 %copy-start.38 = (f32[384]{0:T(512)}, f32[384]{0:T(512)S(1)}, u32[]{:S(2)}) copy-start(f32[384]{0:T(512)S(1)} %get-tuple-element.77) | copy-start | bytes 4612
  20.1 15.4 %copy-start.40 = (f32[384]{0:T(512)}, f32[384]{0:T(512)S(1)}, u32[]{:S(2)}) copy-start(f32[384]{0:T(512)S(1)} %get-tuple-element.78) | copy-start | bytes 4612
  20.1 15.4 %copy-start.42 = (f32[384]{0:T(512)}, f32[384]{0:T(512)S(1)}, u32[]{:S(2)}) copy-start(f32[384]{0:T(512)S(1)} %get-tuple-element.79) | copy-start | bytes 4612
  20.1 15.4 %copy-start.44 = (f32[384]{0:T(512)}, f32[384]{0:T(512)S(1)}, u32[]{:S(2)}) copy-start(f32[384]{0:T(512)S(1)} %get-tuple-element.80) | copy-start | bytes 4612
  22.8 3.4 %copy-start.78 = (s32[1024]{0:T(1024)}, s32[1024]{0:T(1024)S(1)}, u32[]{:S(2)}) copy-start(s32[1024]{0:T(1024)S(1)} %pad_clamp_fusion.3) | copy-start | bytes 12292
  22.8 3.4 %copy-start.77 = (s32[1024]{0:T(1024)}, s32[1024]{0:T(1024)S(1)}, u32[]{:S(2)}) copy-start(s32[1024]{0:T(1024)S(1)} %pad_clamp_fusion.4) | copy-start | bytes 12292
  22.9 10.5 %copy-start.73 = (s32[1024]{0:T(1024)}, s32[1024]{0:T(1024)S(1)}, u32[]{:S(2)}) copy-start(s32[1024]{0:T(1024)S(1)} %pad_clamp_fusion.5) | copy-start | bytes 12292
  22.9 10.5 %copy-start.74 = (s32[1024]{0:T(1024)}, s32[1024]{0:T(1024)S(1)}, u32[]{:S(2)}) copy-start(s32[1024]{0:T(1024)S(1)} %pad_clamp_fusion.6) | copy-start | bytes 12292
  22.9 10.5 %copy-start.75 = (s32[1024]{0:T(1024)}, s32[1024]{0:T(1024)S(1)}, u32[]{:S(2)}) copy-start(s32[1024]{0:T(1024)S(1)} %pad_clamp_fusion.7) | copy-start | bytes 12292
  22.9 10.5 %copy-start.71 = (s32[1024]{0:T(1024)}, s32[1024]{0:T(1024)S(1)}, u32[]{:S(2)}) copy-start(s32[1024]{0:T(1024)S(1)} %pad_clamp_fusion) | copy-start | bytes 12292
  23.0 10.6 %copy-start.72 = (s32[1024]{0:T(1024)}, s32[1024]{0:T(1024)S(1)}, u32[]{:S(2)}) copy-start(s32[1024]{0:T(1024)S(1)} %pad_clamp_fusion.1) | copy-start | bytes 12292
  26.9 8.0 %copy-start.1 = (bf16[1,4,8,8,384]{4,3,2,1,0:T(8,128)(2,1)S(1)}, bf16[1,4,8,8,384]{4,3,2,1,0:T(8,128)(2,1)}, u32[]{:S(2)}) copy-start(bf16[1,4,8,8,384]{4,3,2,1,0:T(8,128)(2,1)} %param.19) | copy-start | bytes 589828
  29.3 6.0 %copy-start.76 = (s32[1024]{0:T(1024)}, s32[1024]{0:T(1024)S(1)}, u32[]{:S(2)}) copy-start(s32[1024]{0:T(1024)S(1)} %pad_clamp_fusion.2) | copy-start | bytes 12292
  32.8 2.7 %copy-start.46 = (f32[384]{0:T(512)S(1)}, f32[384]{0:T(512)}, u32[]{:S(2)}) copy-start(f32[384]{0:T(512)} %get-tuple-element.81) | copy-start | bytes 4612
  32.8 2.7 %copy-start.48 = (f32[384]{0:T(512)S(1)}, f32[384]{0:T(512)}, u32[]{:S(2)}) copy-start(f32[384]{0:T(512)} %get-tuple-element.82) | copy-start | bytes 4612
  32.8 2.7 %copy-start.50 = (f32[384]{0:T(512)S(1)}, f32[384]{0:T(512)}, u32[]{:S(2)}) copy-start(f32[384]{0:T(512)} %get-tuple-element.83) | copy-start | bytes 4612
  35.5 4.5 %copy-start.7 = (f32[384]{0:T(512)S(1)}, f32[384]{0:T(512)}, u32[]{:S(2)}) copy-start(f32[384]{0:T(512)} %param.26) | copy-start | bytes 4612
  45.3 3.1 %copy-start.2 = (f32[256,384]{1,0:T(8,128)}, f32[256,384]{1,0:T(8,128)S(1)}, u32[]{:S(2)}) copy-start(f32[256,384]{1,0:T(8,128)S(1)} %get-tuple-element.151) | copy-start | bytes 1179652
  48.5 134.3 %reduce-scatter.2.cloned.1.call-start = ((), (), s32[]{:S(2)}) async-start(), calls=%async_computation.2 | async-start | bytes 2506752 | tf_op jit(solution)/shard_map/reduce_scatter | solution.py:162
  56.1 114.7 %collective-permute-start.2 = (bf16[4,3,8,384]{3,2,1,0:T(8,128)(2,1)}, bf16[4,3,8,384]{3,2,1,0:T(8,128)(2,1)S(1)}, u32[]{:S(2)}, u32[]{:S(2)}) collective-permute-start(bf16[4,3,8,384]{3,2,1,0:T(8,128)(2,1)} %get-tuple-element.144), channel_id=1, source_target_pairs={{0,1},{1,2},{2,3},{3,4},{4,5},{5,6},{6,7},{7,8},{8,9},{9,10},{10,1... | collective-permute-start | bytes 221192 | tf_op jit(solution)/shard_map/ppermute | solution.py:13
  61.2 111.7 %collective-permute-start.3 = (bf16[4,3,8,384]{3,2,1,0:T(8,128)(2,1)S(1)}, bf16[4,3,8,384]{3,2,1,0:T(8,128)(2,1)S(1)}, u32[]{:S(2)}, u32[]{:S(2)}) collective-permute-start(bf16[4,3,8,384]{3,2,1,0:T(8,128)(2,1)S(1)} %get-tuple-element.145), channel_id=1, source_target_pairs={{1,0},{2,1},{3,2},{4,3},{5,4},{6,5},{7,6},{8,7},{9,8},{10,9},{11,1... | collective-permute-start | bytes 221192 | tf_op jit(solution)/shard_map/ppermute | solution.py:13
  102.3 72.7 %copy-start.90 = (pred[4]{0:T(512)(128)(4,1)S(1)}, pred[4]{0:T(512)(128)(4,1)}, u32[]{:S(2)}) copy-start(pred[4]{0:T(512)(128)(4,1)} %copy-done.89) | copy-start | bytes 16
  170.8 5.0 %copy-start.88 = (pred[4]{0:T(512)(128)(4,1)S(1)}, pred[4]{0:T(512)(128)(4,1)}, u32[]{:S(2)}) copy-start(pred[4]{0:T(512)(128)(4,1)} %copy-done.87) | copy-start | bytes 16
  170.8 5.0 %copy-start.100 = (pred[4]{0:T(512)(128)(4,1)S(1)}, pred[4]{0:T(512)(128)(4,1)}, u32[]{:S(2)}) copy-start(pred[4]{0:T(512)(128)(4,1)} %copy-done.99) | copy-start | bytes 16
  170.8 5.1 %copy-start.86 = (pred[4]{0:T(512)(128)(4,1)S(1)}, pred[4]{0:T(512)(128)(4,1)}, u32[]{:S(2)}) copy-start(pred[4]{0:T(512)(128)(4,1)} %copy-done.85) | copy-start | bytes 16
  170.8 5.1 %copy-start.98 = (pred[4]{0:T(512)(128)(4,1)S(1)}, pred[4]{0:T(512)(128)(4,1)}, u32[]{:S(2)}) copy-start(pred[4]{0:T(512)(128)(4,1)} %copy-done.97) | copy-start | bytes 16
  170.8 5.2 %copy-start.84 = (pred[4]{0:T(512)(128)(4,1)S(1)}, pred[4]{0:T(512)(128)(4,1)}, u32[]{:S(2)}) copy-start(pred[4]{0:T(512)(128)(4,1)} %copy-done.83) | copy-start | bytes 16
  171.5 5.3 %copy-start.82 = (pred[4]{0:T(512)(128)(4,1)S(1)}, pred[4]{0:T(512)(128)(4,1)}, u32[]{:S(2)}) copy-start(pred[4]{0:T(512)(128)(4,1)} %copy-done.81) | copy-start | bytes 16
  171.6 5.3 %copy-start.96 = (pred[4]{0:T(512)(128)(4,1)S(1)}, pred[4]{0:T(512)(128)(4,1)}, u32[]{:S(2)}) copy-start(pred[4]{0:T(512)(128)(4,1)} %copy-done.95) | copy-start | bytes 16
  172.3 4.7 %copy-start.80 = (pred[4]{0:T(512)(128)(4,1)S(1)}, pred[4]{0:T(512)(128)(4,1)}, u32[]{:S(2)}) copy-start(pred[4]{0:T(512)(128)(4,1)} %copy-done.79) | copy-start | bytes 16
  172.3 4.7 %copy-start.94 = (pred[4]{0:T(512)(128)(4,1)S(1)}, pred[4]{0:T(512)(128)(4,1)}, u32[]{:S(2)}) copy-start(pred[4]{0:T(512)(128)(4,1)} %copy-done.93) | copy-start | bytes 16
  (54 other events, 59.8 us)
Sparse Core Ops, SparseCore 0:
  48.6 47.5 all-reduce.3
  100.6 63.7 reduce-scatter.1
where the time goes:
time: 191 us; the launch traced here: 190 us
  blocking collectives  68.5 us (36%)
  other arithmetic  31.7 us (17%)
  waiting for transfers between devices  31.3 us (16%)
  local copies, waits for them, and re-layouts  19.6 us (10%)
  between operations  17.1 us (9%)
  matrix products  11 us (6%)
  starting transfers between devices  10.4 us (5%)
    psum x1, blocking collectives, per_device(): embedding = lax.psum(emb_term, 'space')  61 us
    psum x1, waiting for transfers between devices, per_device(): lax.psum(local_weight.astype(jnp.bfloat16), 'dp').astype(jnp.float32)  31.3 us
    gather x16, local copies, waits for them, and re-layouts, pick(): chosen = jnp.take(source, index, axis=0)  10.5 us
    ppermute x4, starting transfers between devices, passed_along(): lax.ppermute(value, axis, [(source, source + steps) for source in range(l...  10.3 us
    psum x1, blocking collectives, per_device(): lax.psum(kernel_grad.astype(jnp.bfloat16), 'dp').astype(jnp.float32)  7.44 us
    select_n x16, other arithmetic, pick(): return jnp.where(valid[:, None, None, None], chosen, jnp.zeros_like(chosen))  6.9 us
    slice x3, local copies, waits for them, and re-layouts, depthwise(): total = total + window * kernel[row_tap, col_tap]  4.74 us
    broadcast_in_dim x1, other arithmetic, per_device(): return (embedding[None, :], grad_tiles[None], weight_share, kernel_total)  4.44 us
  transfers between devices with their start and end apart: 6, of which 1 were waited for; matrix products, arithmetic and copies ran while one was open for 24% of the time, Pallas kernels for 0%

commit v1 on v0

--- a/solution.py
+++ b/solution.py
@@ -2,6 +2,7 @@
 import jax.numpy as jnp
 from jax import lax
 from jax.sharding import PartitionSpec as P
+from jax.lax import all_gather
 
 sqrt_half = 0.7071067811865476
 inv_root_two_pi = 0.3989422804014327
@@ -116,6 +117,11 @@
     w_out,
     layer_scale,
 ):
+
+    def region_manage(xin, axis_key):
+        f_next = jnp.sum(all_gather(xin, axis_key), axis=0)
+        return f_next
+
     own = tiles_in[0]
     capacity = own.shape[0]
     tile_side = own.shape[1]
@@ -151,7 +157,7 @@
         w_out,
         layer_scale,
     )
-    embedding = lax.psum(emb_term, "space")
+    embedding = region_manage(emb_term, "space")
     local_weight = lax.dot_general(
         activated, grad_mixed, (((0,), (0,)), ((), ())), preferred_element_type=jnp.float32
     )

time: 191 us -> 239 us (1.25)
  blocking collectives: 68.5 us -> 88.6 us
  other arithmetic: 31.7 us -> 41.9 us
  local copies, waits for them, and re-layouts: 19.6 us -> 29 us
  waiting for transfers between devices: 31.3 us -> 40.1 us
    all_gather x0 -> x1, blocking collectives: none -> 21.9 us  [region_manage(): f_next = jnp.sum(all_gather(xin, axis_key), axis=0)]
    psum x1, waiting for transfers between devices: 31.3 us -> 40.1 us  [per_device(): lax.psum(local_weight.astype(jnp.bfloat16), 'dp').astype(jnp.float32)]
    select_n x16, other arithmetic: 6.9 us -> 12 us  [pick(): return jnp.where(valid[:, None, None, None], chosen, jnp.zeros_like(chosen))]
    gather x8, other arithmetic: 0.05 us -> 3.58 us
    another operation x50, local copies, waits for them, and re-layouts: 0.48 us -> 3.74 us  [block_pass(): kernel_grad = jnp.stack(kernel_rows).reshape(7, 7, channels)]
    reduce_sum x3, other arithmetic: 2.17 us -> 4.95 us  [block_pass(): kernel_rows.append(jnp.sum(window * grad_conv, axis=(0, 1, 2)))]
    gather x16, local copies, waits for them, and re-layouts: 10.5 us -> 13 us  [pick(): chosen = jnp.take(source, index, axis=0)]
where the time goes in v1:
time: 239 us; the launch traced here: 238 us
  blocking collectives  88.6 us (37%)
  other arithmetic  41.9 us (18%)
  waiting for transfers between devices  40.1 us (17%)
  local copies, waits for them, and re-layouts  29 us (12%)
  between operations  17.3 us (7%)
  matrix products  11.8 us (5%)
  starting transfers between devices  8.9 us (4%)
    psum x1, blocking collectives, per_device(): kernel_total = lax.psum(kernel_dp, 'space')  59.3 us
    psum x1, waiting for transfers between devices, per_device(): lax.psum(local_weight.astype(jnp.bfloat16), 'dp').astype(jnp.float32)  40.1 us
    all_gather x1, blocking collectives, region_manage(): f_next = jnp.sum(all_gather(xin, axis_key), axis=0)  21.9 us
    gather x16, local copies, waits for them, and re-layouts, pick(): chosen = jnp.take(source, index, axis=0)  13 us
    select_n x16, other arithmetic, pick(): return jnp.where(valid[:, None, None, None], chosen, jnp.zeros_like(chosen))  12 us
    ppermute x4, starting transfers between devices, passed_along(): lax.ppermute(value, axis, [(source, source + steps) for source in range(l...  8.82 us
    psum x1, blocking collectives, per_device(): lax.psum(kernel_grad.astype(jnp.bfloat16), 'dp').astype(jnp.float32)  7.44 us
    reduce_sum x3, other arithmetic, block_pass(): kernel_rows.append(jnp.sum(window * grad_conv, axis=(0, 1, 2)))  4.95 us
  transfers between devices with their start and end apart: 6, of which 1 were waited for; matrix products, arithmetic and copies ran while one was open for 24% of the time, Pallas kernels for 0%

profile of v1, /device:TPU:0, one launch (start us, length us, event | category | flops | bytes accessed | tf_op | source)
XLA Modules:
  0.0 237.6 jit_solution(13310036319751499531)
XLA Ops:
  7.3 1.1 fusion.190
  8.3 1.3 collective-permute-start.1
  9.6 3.0 %collective-permute-start = (bf16[4,3,8,384]{3,2,1,0:T(8,128)(2,1)S(1)}, bf16[4,3,8,384]{3,2,1,0:T(8,128)(2,1)S(1)}, u32[]{:S(2)}, u32[]{:S(2)}) collective-permute-start(bf16[4,3,8,384]{3,2,1,0:T(8,128)(2,1)S(1)} %get-tuple-element.144), channel_id=1, source_target_pairs={{0,1},{1,2},{2,3},{3,4},{4,5},{5,6},{6,7},{7,8},{8,9},{9,10},{10,1... | collective-permute-start | bytes 221192 | tf_op jit(solution)/shard_map/ppermute | solution.py:14
  12.7 1.1 fusion.191
  13.8 1.9 compare_reduce_fusion.7
  15.6 1.3 clamp_reduce_fusion.7
  19.3 1.3 slice_reduce_fusion.47
  20.7 1.8 slice_reduce_fusion.48
  22.6 1.6 slice_reduce_fusion.46
  28.5 0.7 mul.1256
  29.3 0.6 gather_fusion.3
  31.3 0.7 select_select_fusion.5
  32.1 0.8 select_select_fusion.4
  32.9 0.8 fusion.169
  34.3 0.7 gather_fusion.6
  35.0 0.7 select_select_fusion.6
  35.7 0.7 gather_fusion.1
  36.4 0.8 select_select_fusion.7
  37.2 0.7 gather_fusion.7
  37.9 0.7 fusion.180
  38.6 0.7 gather_fusion.2
  39.3 0.7 fusion.182
  40.0 0.7 gather_fusion.5
  40.7 0.8 fusion.181
  41.5 0.7 gather_fusion
  42.2 0.8 fusion.183
  43.8 4.1 %fusion.186 = (f32[4,8,8]{2,1,0:T(8,128)S(1)}, f32[4,8,8,384]{3,2,1,0:T(8,128)S(1)}) fusion(f32[384]{0:T(512)} %get-tuple-element.114, bf16[4,11,14,384]{3,2,1,0:T(8,128)(2,1)S(1)} %get-tuple-element.141, f32[384]{0:T(512)} %get-tuple-element.115, f32[384]{0:T(512)S(1)} %get-tuple-element.68, f32[384]{0:T(512)S(1)} %get-tuple-element.69, ...), kind=kLoop, calls=%fused_computation.494 | loop fusion | flops 16219904 | bytes 9071104 | tf_op jit(solution)/shard_map/reduce_sum | solution.py:68
  48.3 2.0 multiply_convert_fusion
  50.3 3.1 %multiply_reduce_fusion.1 = (f32[256]{0:T(256)S(1)}, f32[256,384]{1,0:T(8,128)S(1)}) fusion(f32[384]{0:T(512)S(1)} %copy-done.10, bf16[384,1536]{1,0:T(8,128)(2,1)S(1)} %copy-done, bf16[256,384]{1,0:T(8,128)(2,1)S(1)} %copy-done.6, bf16[1536,384]{1,0:T(8,128)(2,1)} %param.28, f32[256,1536]{1,0:T(8,128)} %get-tuple-element.151), kind=kOutput, calls=%fused_computation.359 | convolution fusion | flops 608108288 | bytes 4524544 | tf_op jit(solution)/shard_map/dot_general | solution.py:87
  54.2 2.7 %convolution_convert_fusion = bf16[1536,384]{1,0:T(8,128)(2,1)} fusion(bf16[256,1536]{1,0:T(8,128)(2,1)} %get-tuple-element.150, bf16[256,384]{1,0:T(8,128)(2,1)S(1)} %copy-done.6), kind=kOutput, calls=%fused_computation.16 | convolution fusion | flops 302579712 | bytes 2162688 | tf_op jit(solution)/shard_map/dot_general | solution.py:161
  57.1 0.7 div.36
  57.7 2.5 %fusion.103 = (bf16[384]{0:T(512)(128)(2,1)}, bf16[384]{0:T(512)(128)(2,1)}, bf16[384]{0:T(512)(128)(2,1)}, bf16[384]{0:T(512)(128)(2,1)}, bf16[384]{0:T(512)(12...) fusion(bf16[4,11,14,384]{3,2,1,0:T(8,128)(2,1)S(1)} %get-tuple-, ...), kind=kLoop, calls=%fused_computation.243 | loop fusion | flops 5989632 | bytes 4738048 | tf_op jit(solution)/shard_map/reduce_sum | solution.py:102
  60.3 0.8 fusion.188
  61.1 2.2 fusion.53
  63.3 40.1 %all-reduce.3.cloned.1.call-done = bf16[1536,384]{1,0:T(8,128)(2,1)} async-done(((bf16[1536,384]{1,0:T(8,128)(2,1)}), bf16[1536,384]{1,0:T(8,128)(2,1)}) %all-reduce.3.cloned.1.call-update) | async-done | bytes 1179664 | tf_op jit(solution)/shard_map/psum | solution.py:165
  103.4 2.8 %convert_element_type.315 = f32[1536,384]{1,0:T(8,128)} convert(bf16[1536,384]{1,0:T(8,128)(2,1)} %all-reduce.3.cloned.1.call-done) | non-fusion elementwise | flops 589824 | bytes 3538944 | tf_op jit(solution)/shard_map/convert_element_type | solution.py:165
  106.3 1.7 fusion.189
  108.0 4.0 %fusion.85 = (bf16[384]{0:T(512)(128)(2,1)}, bf16[384]{0:T(512)(128)(2,1)}, bf16[384]{0:T(512)(128)(2,1)}, bf16[384]{0:T(512)(128)(2,1)}, bf16[384]{0:T(512)(128...) fusion(f32[4,8,8,384]{3,2,1,0:T(8,128)S(1)} %get-tuple-element., ...), kind=kOutput, calls=%fused_computation.225 | convolution fusion | flops 306998016 | bytes 3505152 | tf_op jit(solution)/shard_map/dot_general | solution.py:75
  112.0 1.3 collective-permute-start.3
  113.2 3.2 %collective-permute-start.2 = (bf16[4,3,8,384]{3,2,1,0:T(8,128)(2,1)}, bf16[4,3,8,384]{3,2,1,0:T(8,128)(2,1)S(1)}, u32[]{:S(2)}, u32[]{:S(2)}) collective-permute-start(bf16[4,3,8,384]{3,2,1,0:T(8,128)(2,1)} %get-tuple-element.142), channel_id=1, source_target_pairs={{0,1},{1,2},{2,3},{3,4},{4,5},{5,6},{6,7},{7,8},{8,9},{9,10},{10,1... | collective-permute-start | bytes 221192 | tf_op jit(solution)/shard_map/ppermute | solution.py:14
  116.5 1.7 gather_fusion.11
  118.6 1.7 gather_fusion.12
  120.4 0.7 multiply_reduce_fusion.3
  121.1 0.7 select_select_fusion.1
  121.8 0.8 select_select_fusion
  124.7 0.7 stack.233
  125.3 0.7 stack.234
  126.0 0.7 stack.235
  127.2 7.4 %psum.22 = bf16[7,7,384]{2,1,0:T(8,128)(2,1)S(1)} all-reduce(bf16[7,7,384]{2,1,0:T(8,128)(2,1)S(1)} %convert_element_type.316), channel_id=1, replica_groups=mesh['dp'=2,'space'=16] {'dp'}, use_global_device_ids=true, to_apply=%region_58.63 | all-reduce | flops 18816 | bytes 75264 | tf_op jit(solution)/shard_map/psum | solution.py:166
  134.7 21.9 %all-gather.1 = f32[16,1,384]{2,1,0:T(1,128)S(1)} all-gather(f32[1,1,384]{2,1,0:T(1,128)S(1)} %reshape.470), channel_id=2, replica_groups=mesh['dp'=2,'space'=16] {'space'}, dimensions={0}, use_global_device_ids=true | all-gather | bytes 26112 | tf_op jit(solution)/shard_map/all_gather | solution.py:122
  157.2 59.3 %all-reduce.4 = f32[7,7,384]{2,1,0:T(8,128)} all-reduce(bf16[7,7,384]{2,1,0:T(8,128)(2,1)S(1)} %psum.22), channel_id=1, replica_groups=mesh['dp'=2,'space'=16] {'space'}, use_global_device_ids=true, to_apply=%region_59.64 | all-reduce | flops 18816 | bytes 112896 | tf_op jit(solution)/shard_map/psum | solution.py:169
  216.5 0.7 gather_fusion.14
  217.2 0.7 gather_fusion.15
  217.9 0.7 gather_fusion.13
  218.6 0.7 gather_fusion.9
  219.3 0.7 gather_fusion.8
  219.9 0.7 gather_fusion.10
  220.6 0.7 fusion.176
  221.3 0.8 fusion.177
  222.1 0.8 fusion.179
  222.9 0.7 fusion.178
  223.6 0.8 select_select_fusion.2
  224.3 0.8 select_select_fusion.3
  226.4 4.4 %fusion.175 = bf16[1,4,8,8,384]{4,3,2,1,0:T(8,128)(2,1)} fusion(f32[384]{0:T(512)S(1)} %copy-done.50, f32[4,11,14,384]{3,2,1,0:T(8,128)S(1)} %get-tuple-element.136, f32[384]{0:T(512)S(1)} %copy-done.12, f32[384]{0:T(512)} %get-tuple-element.105, f32[384]{0:T(512)} %get-tuple-element.113, f32[384]{0:T(512)} %get-tuple-element.112, ...), kind=kLoop, calls=%fused_computation.371 | loop fusion | flops 10715136 | bytes 17677840 | tf_op jit(solution)/shard_map/broadcast_in_dim | solution.py:189
  (358 shorter events, 13.2 us)
Async XLA Ops:
  7.2 41.1 %copy-start = (bf16[384,1536]{1,0:T(8,128)(2,1)S(1)}, bf16[384,1536]{1,0:T(8,128)(2,1)}, u32[]{:S(2)}) copy-start(bf16[384,1536]{1,0:T(8,128)(2,1)} %param.27) | copy-start | bytes 3538948
  7.2 23.5 %copy-start.129 = (f32[1,384]{1,0:T(1,128)S(1)}, f32[1,384]{1,0:T(1,128)}, u32[]{:S(2)}) copy-start(f32[1,384]{1,0:T(1,128)} %param.22) | copy-start | bytes 4612
  7.2 23.5 %copy-start.130 = (f32[1,4]{1,0:T(1,128)S(1)}, f32[1,4]{1,0:T(1,128)}, u32[]{:S(2)}) copy-start(f32[1,4]{1,0:T(1,128)} %param.21) | copy-start | bytes 52
  7.2 25.7 %copy-start.4 = (bf16[1,4,8,8,384]{4,3,2,1,0:T(8,128)(2,1)S(1)}, bf16[1,4,8,8,384]{4,3,2,1,0:T(8,128)(2,1)}, u32[]{:S(2)}) copy-start(bf16[1,4,8,8,384]{4,3,2,1,0:T(8,128)(2,1)} %param.20) | copy-start | bytes 589828
  7.2 25.7 %copy-start.85 = (f32[384]{0:T(512)S(1)}, f32[384]{0:T(512)}, u32[]{:S(2)}) copy-start(f32[384]{0:T(512)} %param.29) | copy-start | bytes 4612
  7.2 96.2 %all-reduce.3.cloned.1.call-start = ((), (), s32[]{:S(2)}) async-start(), calls=%async_computation.1 | async-start | bytes 2359296 | tf_op jit(solution)/shard_map/psum | solution.py:165
  8.3 25.9 %collective-permute-start.1 = (bf16[4,3,8,384]{3,2,1,0:T(8,128)(2,1)S(1)}, bf16[4,3,8,384]{3,2,1,0:T(8,128)(2,1)S(1)}, u32[]{:S(2)}, u32[]{:S(2)}) collective-permute-start(bf16[4,3,8,384]{3,2,1,0:T(8,128)(2,1)S(1)} %get-tuple-element.145), channel_id=1, source_target_pairs={{1,0},{2,1},{3,2},{4,3},{5,4},{6,5},{7,6},{8,7},{9,8},{10,9},{11,1... | collective-permute-start | bytes 221192 | tf_op jit(solution)/shard_map/ppermute | solution.py:14
  9.6 26.1 %collective-permute-start = (bf16[4,3,8,384]{3,2,1,0:T(8,128)(2,1)S(1)}, bf16[4,3,8,384]{3,2,1,0:T(8,128)(2,1)S(1)}, u32[]{:S(2)}, u32[]{:S(2)}) collective-permute-start(bf16[4,3,8,384]{3,2,1,0:T(8,128)(2,1)S(1)} %get-tuple-element.144), channel_id=1, source_target_pairs={{0,1},{1,2},{2,3},{3,4},{4,5},{5,6},{6,7},{7,8},{8,9},{9,10},{10,1... | collective-permute-start | bytes 221192 | tf_op jit(solution)/shard_map/ppermute | solution.py:14
  20.5 22.9 %copy-start.11 = (f32[384]{0:T(512)}, f32[384]{0:T(512)S(1)}, u32[]{:S(2)}) copy-start(f32[384]{0:T(512)S(1)} %get-tuple-element.86) | copy-start | bytes 4612
  20.5 22.9 %copy-start.13 = (f32[384]{0:T(512)}, f32[384]{0:T(512)S(1)}, u32[]{:S(2)}) copy-start(f32[384]{0:T(512)S(1)} %get-tuple-element.87) | copy-start | bytes 4612
  20.5 22.9 %copy-start.15 = (f32[384]{0:T(512)}, f32[384]{0:T(512)S(1)}, u32[]{:S(2)}) copy-start(f32[384]{0:T(512)S(1)} %get-tuple-element.88) | copy-start | bytes 4612
  20.5 22.9 %copy-start.17 = (f32[384]{0:T(512)}, f32[384]{0:T(512)S(1)}, u32[]{:S(2)}) copy-start(f32[384]{0:T(512)S(1)} %get-tuple-element.89) | copy-start | bytes 4612
  20.6 22.9 %copy-start.19 = (f32[384]{0:T(512)}, f32[384]{0:T(512)S(1)}, u32[]{:S(2)}) copy-start(f32[384]{0:T(512)S(1)} %get-tuple-element.90) | copy-start | bytes 4612
  20.6 22.9 %copy-start.21 = (f32[384]{0:T(512)}, f32[384]{0:T(512)S(1)}, u32[]{:S(2)}) copy-start(f32[384]{0:T(512)S(1)} %get-tuple-element.91) | copy-start | bytes 4612
  20.6 22.9 %copy-start.23 = (f32[384]{0:T(512)}, f32[384]{0:T(512)S(1)}, u32[]{:S(2)}) copy-start(f32[384]{0:T(512)S(1)} %get-tuple-element.92) | copy-start | bytes 4612
  20.6 22.9 %copy-start.25 = (f32[384]{0:T(512)}, f32[384]{0:T(512)S(1)}, u32[]{:S(2)}) copy-start(f32[384]{0:T(512)S(1)} %get-tuple-element.93) | copy-start | bytes 4612
  20.6 22.9 %copy-start.27 = (f32[384]{0:T(512)}, f32[384]{0:T(512)S(1)}, u32[]{:S(2)}) copy-start(f32[384]{0:T(512)S(1)} %get-tuple-element.94) | copy-start | bytes 4612
  20.6 22.9 %copy-start.29 = (f32[384]{0:T(512)}, f32[384]{0:T(512)S(1)}, u32[]{:S(2)}) copy-start(f32[384]{0:T(512)S(1)} %get-tuple-element.95) | copy-start | bytes 4612
  20.6 22.9 %copy-start.31 = (f32[384]{0:T(512)}, f32[384]{0:T(512)S(1)}, u32[]{:S(2)}) copy-start(f32[384]{0:T(512)S(1)} %get-tuple-element.96) | copy-start | bytes 4612
  20.6 22.9 %copy-start.33 = (f32[384]{0:T(512)}, f32[384]{0:T(512)S(1)}, u32[]{:S(2)}) copy-start(f32[384]{0:T(512)S(1)} %get-tuple-element.97) | copy-start | bytes 4612
  20.6 22.9 %copy-start.35 = (f32[384]{0:T(512)}, f32[384]{0:T(512)S(1)}, u32[]{:S(2)}) copy-start(f32[384]{0:T(512)S(1)} %get-tuple-element.98) | copy-start | bytes 4612
  20.6 22.9 %copy-start.37 = (f32[384]{0:T(512)}, f32[384]{0:T(512)S(1)}, u32[]{:S(2)}) copy-start(f32[384]{0:T(512)S(1)} %get-tuple-element.99) | copy-start | bytes 4612
  20.7 22.9 %copy-start.39 = (f32[384]{0:T(512)}, f32[384]{0:T(512)S(1)}, u32[]{:S(2)}) copy-start(f32[384]{0:T(512)S(1)} %get-tuple-element.100) | copy-start | bytes 4612
  20.7 22.9 %copy-start.41 = (f32[384]{0:T(512)}, f32[384]{0:T(512)S(1)}, u32[]{:S(2)}) copy-start(f32[384]{0:T(512)S(1)} %get-tuple-element.101) | copy-start | bytes 4612
  20.7 22.9 %copy-start.43 = (f32[384]{0:T(512)}, f32[384]{0:T(512)S(1)}, u32[]{:S(2)}) copy-start(f32[384]{0:T(512)S(1)} %get-tuple-element.102) | copy-start | bytes 4612
  20.7 22.9 %copy-start.45 = (f32[384]{0:T(512)}, f32[384]{0:T(512)S(1)}, u32[]{:S(2)}) copy-start(f32[384]{0:T(512)S(1)} %get-tuple-element.103) | copy-start | bytes 4612
  20.7 22.9 %copy-start.47 = (f32[384]{0:T(512)}, f32[384]{0:T(512)S(1)}, u32[]{:S(2)}) copy-start(f32[384]{0:T(512)S(1)} %get-tuple-element.104) | copy-start | bytes 4612
  22.5 21.1 %copy-start.49 = (f32[384]{0:T(512)}, f32[384]{0:T(512)S(1)}, u32[]{:S(2)}) copy-start(f32[384]{0:T(512)S(1)} %get-tuple-element.67) | copy-start | bytes 4612
  22.5 21.1 %copy-start.51 = (f32[384]{0:T(512)}, f32[384]{0:T(512)S(1)}, u32[]{:S(2)}) copy-start(f32[384]{0:T(512)S(1)} %get-tuple-element.68) | copy-start | bytes 4612
  22.5 21.1 %copy-start.53 = (f32[384]{0:T(512)}, f32[384]{0:T(512)S(1)}, u32[]{:S(2)}) copy-start(f32[384]{0:T(512)S(1)} %get-tuple-element.69) | copy-start | bytes 4612
  22.5 21.1 %copy-start.55 = (f32[384]{0:T(512)}, f32[384]{0:T(512)S(1)}, u32[]{:S(2)}) copy-start(f32[384]{0:T(512)S(1)} %get-tuple-element.70) | copy-start | bytes 4612
  22.5 21.1 %copy-start.57 = (f32[384]{0:T(512)}, f32[384]{0:T(512)S(1)}, u32[]{:S(2)}) copy-start(f32[384]{0:T(512)S(1)} %get-tuple-element.71) | copy-start | bytes 4612
  22.5 21.1 %copy-start.59 = (f32[384]{0:T(512)}, f32[384]{0:T(512)S(1)}, u32[]{:S(2)}) copy-start(f32[384]{0:T(512)S(1)} %get-tuple-element.72) | copy-start | bytes 4612
  22.5 21.1 %copy-start.61 = (f32[384]{0:T(512)}, f32[384]{0:T(512)S(1)}, u32[]{:S(2)}) copy-start(f32[384]{0:T(512)S(1)} %get-tuple-element.73) | copy-start | bytes 4612
  22.5 21.1 %copy-start.63 = (f32[384]{0:T(512)}, f32[384]{0:T(512)S(1)}, u32[]{:S(2)}) copy-start(f32[384]{0:T(512)S(1)} %get-tuple-element.74) | copy-start | bytes 4612
  22.5 21.1 %copy-start.65 = (f32[384]{0:T(512)}, f32[384]{0:T(512)S(1)}, u32[]{:S(2)}) copy-start(f32[384]{0:T(512)S(1)} %get-tuple-element.75) | copy-start | bytes 4612
  22.5 21.1 %copy-start.67 = (f32[384]{0:T(512)}, f32[384]{0:T(512)S(1)}, u32[]{:S(2)}) copy-start(f32[384]{0:T(512)S(1)} %get-tuple-element.76) | copy-start | bytes 4612
  22.6 21.1 %copy-start.69 = (f32[384]{0:T(512)}, f32[384]{0:T(512)S(1)}, u32[]{:S(2)}) copy-start(f32[384]{0:T(512)S(1)} %get-tuple-element.77) | copy-start | bytes 4612
  22.6 21.1 %copy-start.71 = (f32[384]{0:T(512)}, f32[384]{0:T(512)S(1)}, u32[]{:S(2)}) copy-start(f32[384]{0:T(512)S(1)} %get-tuple-element.78) | copy-start | bytes 4612
  22.6 21.1 %copy-start.73 = (f32[384]{0:T(512)}, f32[384]{0:T(512)S(1)}, u32[]{:S(2)}) copy-start(f32[384]{0:T(512)S(1)} %get-tuple-element.79) | copy-start | bytes 4612
  22.6 21.1 %copy-start.75 = (f32[384]{0:T(512)}, f32[384]{0:T(512)S(1)}, u32[]{:S(2)}) copy-start(f32[384]{0:T(512)S(1)} %get-tuple-element.80) | copy-start | bytes 4612
  22.6 21.1 %copy-start.77 = (f32[384]{0:T(512)}, f32[384]{0:T(512)S(1)}, u32[]{:S(2)}) copy-start(f32[384]{0:T(512)S(1)} %get-tuple-element.81) | copy-start | bytes 4612
  22.6 21.1 %copy-start.79 = (f32[384]{0:T(512)}, f32[384]{0:T(512)S(1)}, u32[]{:S(2)}) copy-start(f32[384]{0:T(512)S(1)} %get-tuple-element.82) | copy-start | bytes 4612
  22.6 21.1 %copy-start.81 = (f32[384]{0:T(512)}, f32[384]{0:T(512)S(1)}, u32[]{:S(2)}) copy-start(f32[384]{0:T(512)S(1)} %get-tuple-element.83) | copy-start | bytes 4612
  22.6 21.1 %copy-start.83 = (f32[384]{0:T(512)}, f32[384]{0:T(512)S(1)}, u32[]{:S(2)}) copy-start(f32[384]{0:T(512)S(1)} %get-tuple-element.84) | copy-start | bytes 4612
  30.7 12.3 %copy-start.2 = (bf16[1,4,8,8,384]{4,3,2,1,0:T(8,128)(2,1)S(1)}, bf16[1,4,8,8,384]{4,3,2,1,0:T(8,128)(2,1)}, u32[]{:S(2)}) copy-start(bf16[1,4,8,8,384]{4,3,2,1,0:T(8,128)(2,1)} %param.19) | copy-start | bytes 589828
  31.3 10.8 %copy-start.8 = (f32[4,384]{1,0:T(4,128)}, f32[4,384]{1,0:T(4,128)S(1)}, u32[]{:S(2)}) copy-start(f32[4,384]{1,0:T(4,128)S(1)} %multiply_multiply_fusion.1) | copy-start | bytes 18436
  32.9 15.0 %copy-start.3 = (bf16[4,8,3,384]{3,2,1,0:T(4,128)(2,1)}, bf16[4,8,3,384]{3,2,1,0:T(4,128)(2,1)S(1)}, u32[]{:S(2)}) copy-start(bf16[4,8,3,384]{3,2,1,0:T(4,128)(2,1)S(1)} %select_select_fusion.4) | copy-start | bytes 221188
  57.0 173.8 %reduce-scatter.2.cloned.1.call-start = ((), (), s32[]{:S(2)}) async-start(), calls=%async_computation.2 | async-start | bytes 2506752 | tf_op jit(solution)/shard_map/reduce_scatter | solution.py:168
  112.0 104.5 %collective-permute-start.3 = (bf16[4,3,8,384]{3,2,1,0:T(8,128)(2,1)}, bf16[4,3,8,384]{3,2,1,0:T(8,128)(2,1)S(1)}, u32[]{:S(2)}, u32[]{:S(2)}) collective-permute-start(bf16[4,3,8,384]{3,2,1,0:T(8,128)(2,1)} %get-tuple-element.143), channel_id=1, source_target_pairs={{1,0},{2,1},{3,2},{4,3},{5,4},{6,5},{7,6},{8,7},{9,8},{10,9},{11,1... | collective-permute-start | bytes 221192 | tf_op jit(solution)/shard_map/ppermute | solution.py:14
  113.2 105.3 %collective-permute-start.2 = (bf16[4,3,8,384]{3,2,1,0:T(8,128)(2,1)}, bf16[4,3,8,384]{3,2,1,0:T(8,128)(2,1)S(1)}, u32[]{:S(2)}, u32[]{:S(2)}) collective-permute-start(bf16[4,3,8,384]{3,2,1,0:T(8,128)(2,1)} %get-tuple-element.142), channel_id=1, source_target_pairs={{0,1},{1,2},{2,3},{3,4},{4,5},{5,6},{6,7},{7,8},{8,9},{9,10},{10,1... | collective-permute-start | bytes 221192 | tf_op jit(solution)/shard_map/ppermute | solution.py:14
  118.5 8.2 %copy-start.128 = (bf16[384]{0:T(512)(128)(2,1)S(1)}, bf16[384]{0:T(512)(128)(2,1)}, u32[]{:S(2)}) copy-start(bf16[384]{0:T(512)(128)(2,1)} %get-tuple-element.20) | copy-start | bytes 2308
  118.5 8.2 %copy-start.127 = (bf16[384]{0:T(512)(128)(2,1)S(1)}, bf16[384]{0:T(512)(128)(2,1)}, u32[]{:S(2)}) copy-start(bf16[384]{0:T(512)(128)(2,1)} %get-tuple-element.19) | copy-start | bytes 2308
  118.5 8.2 %copy-start.126 = (bf16[384]{0:T(512)(128)(2,1)S(1)}, bf16[384]{0:T(512)(128)(2,1)}, u32[]{:S(2)}) copy-start(bf16[384]{0:T(512)(128)(2,1)} %get-tuple-element.18) | copy-start | bytes 2308
  118.5 8.2 %copy-start.125 = (bf16[384]{0:T(512)(128)(2,1)S(1)}, bf16[384]{0:T(512)(128)(2,1)}, u32[]{:S(2)}) copy-start(bf16[384]{0:T(512)(128)(2,1)} %get-tuple-element.17) | copy-start | bytes 2308
  118.5 8.2 %copy-start.124 = (bf16[384]{0:T(512)(128)(2,1)S(1)}, bf16[384]{0:T(512)(128)(2,1)}, u32[]{:S(2)}) copy-start(bf16[384]{0:T(512)(128)(2,1)} %get-tuple-element.16) | copy-start | bytes 2308
  118.5 8.3 %copy-start.123 = (bf16[384]{0:T(512)(128)(2,1)S(1)}, bf16[384]{0:T(512)(128)(2,1)}, u32[]{:S(2)}) copy-start(bf16[384]{0:T(512)(128)(2,1)} %get-tuple-element.15) | copy-start | bytes 2308
  118.5 8.3 %copy-start.122 = (bf16[384]{0:T(512)(128)(2,1)S(1)}, bf16[384]{0:T(512)(128)(2,1)}, u32[]{:S(2)}) copy-start(bf16[384]{0:T(512)(128)(2,1)} %get-tuple-element.14) | copy-start | bytes 2308
  118.5 8.3 %copy-start.121 = (bf16[384]{0:T(512)(128)(2,1)S(1)}, bf16[384]{0:T(512)(128)(2,1)}, u32[]{:S(2)}) copy-start(bf16[384]{0:T(512)(128)(2,1)} %get-tuple-element.13) | copy-start | bytes 2308
  118.6 8.3 %copy-start.120 = (bf16[384]{0:T(512)(128)(2,1)S(1)}, bf16[384]{0:T(512)(128)(2,1)}, u32[]{:S(2)}) copy-start(bf16[384]{0:T(512)(128)(2,1)} %get-tuple-element.12) | copy-start | bytes 2308
  118.6 8.3 %copy-start.119 = (bf16[384]{0:T(512)(128)(2,1)S(1)}, bf16[384]{0:T(512)(128)(2,1)}, u32[]{:S(2)}) copy-start(bf16[384]{0:T(512)(128)(2,1)} %get-tuple-element.11) | copy-start | bytes 2308
  118.6 8.3 %copy-start.118 = (bf16[384]{0:T(512)(128)(2,1)S(1)}, bf16[384]{0:T(512)(128)(2,1)}, u32[]{:S(2)}) copy-start(bf16[384]{0:T(512)(128)(2,1)} %get-tuple-element.10) | copy-start | bytes 2308
  118.6 8.3 %copy-start.117 = (bf16[384]{0:T(512)(128)(2,1)S(1)}, bf16[384]{0:T(512)(128)(2,1)}, u32[]{:S(2)}) copy-start(bf16[384]{0:T(512)(128)(2,1)} %get-tuple-element.9) | copy-start | bytes 2308
  118.6 8.3 %copy-start.116 = (bf16[384]{0:T(512)(128)(2,1)S(1)}, bf16[384]{0:T(512)(128)(2,1)}, u32[]{:S(2)}) copy-start(bf16[384]{0:T(512)(128)(2,1)} %get-tuple-element.8) | copy-start | bytes 2308
  (73 other events, 190.1 us)
Sparse Core Ops, SparseCore 0:
  57.1 46.2 all-reduce.2
  107.8 63.3 reduce-scatter.1
